TPU v7x, 128 devices: a whole 4x4x4 slice. The times are simulated.
128 devices in a mesh: row: 16 (over y, x), col: 8 (over z, core).
Axes of the slice: x: 4, y: 4, z: 4, core: 2. Of those that a mesh axis runs over, the one named last changes fastest.
Arguments:
- src_points: bfloat16 [16384, 256], P('row'), may hold values from -32 to 32, as said below
- tgt_points: bfloat16 [32768, 256], P(('col', 'row')), may hold values from -32 to 32, as said below
- log_src_mass: float32 [16384], P('row'), may hold values from -3 to 3
- log_tgt_mass: float32 [32768], P('col'), may hold values from -3 to 3
Outputs:
- src_potential: float32 [16384], P('row')
- tgt_potential: float32 [32768], P('col')
- mean_potentials: float32 [], replicated
Inputs may be any that keep to these rules, and one draw needn't show every extreme that they name: `src_points`: point coordinates. `tgt_points`: point coordinates.
All inputs are finite; a program needn't handle non-finite values.
Results may differ from a plain program's by a relative error of at most 0.0003.
Values may be sent and summed in bfloat16 or wider, within the bound.
No kernel may reach another device: no remote copies, remote signals or barrier semaphores. Data moves between devices by JAX's collectives and lax.ppermute only.
A program may use at most 64 MiB of HBM per device.

v0:
```python
import jax
import jax.numpy as jnp
from jax import lax
from jax.sharding import Mesh
from jax.sharding import PartitionSpec as P

ITERS = 3
ROW = ("row_0", "row_1")
COL = ("col_0", "col_1")
ROW_COL = ("row_0", "row_1", "col_0", "col_1")
COL_ROW = ("col_0", "col_1", "row_0", "row_1")
entropy_weight = 0.1


def from_everyone(value, axis):
    peers = lax.axis_size(axis)
    return lax.all_to_all(
        jnp.broadcast_to(value[None], (peers, *value.shape)), axis, 0, 0, tiled=True
    )


def laid_out(tiles, dim):
    shape = list(tiles.shape[1:])
    shape[dim] *= tiles.shape[0]
    return jnp.moveaxis(tiles, 0, dim).reshape(shape)


def gathered_copies(value, axis, dim):
    tiles = from_everyone(value, axis)
    return laid_out(tiles, dim)


def collected_together(value, axis):
    leaves = jax.tree.leaves(value)
    sequence = sorted(range(len(leaves)), key=lambda k: -leaves[k].size)
    width = (1, *leaves[sequence[0]].shape)[-1]
    lines = [
        jnp.pad(leaves[k].reshape(-1), (0, -leaves[k].size % width)).reshape(-1, width)
        for k in sequence
    ]
    both, at, found = (from_everyone(jnp.concatenate(lines), axis), 0, {})
    for k, line in zip(sequence, lines):
        section = both[:, at : at + len(line)].reshape(len(both), -1)
        found[k] = section[:, : leaves[k].size].reshape(-1, *leaves[k].shape)
        at += len(line)
    numbers = iter(range(len(leaves)))
    return jax.tree.map(lambda _: found[next(numbers)], value)


def once_a_type(value, axis):
    leaves, found = (jax.tree.leaves(value), {})
    for leading, a in enumerate(leaves):
        if leading not in found:
            alike = [k for k, b in enumerate(leaves) if b.dtype == a.dtype]
            got = (
                collected_together([leaves[k] for k in alike], axis)
                if len(alike) > 1
                else [from_everyone(a, axis)]
            )
            for k, b in zip(alike, got):
                found[k] = b
    numbers = iter(range(len(leaves)))
    return jax.tree.map(lambda _: found[next(numbers)], value)


def folded_in_pairs(pieces, combine):
    while len(jax.tree.leaves(pieces)[0]) > 1:
        pieces = jax.vmap(combine)(
            *(jax.tree.map(lambda part: part[side::2], pieces) for side in (0, 1))
        )
    return jax.tree.map(lambda part: part[0], pieces)


def combined_all(value, axis, combine):
    pieces = once_a_type(value, axis)
    return folded_in_pairs(pieces, combine)


def joined_all(value, axis, combine):
    pieces = collected_together(value, axis)
    return folded_in_pairs(pieces, combine)


def over_axes(value, axes):
    for axis in axes:
        value = lax.psum(value, axis)
    return value


def cost_block(points_a, squares_a, points_b, squares_b):
    product = lax.dot_general(
        points_a, points_b, (((1,), (1,)), ((), ())), preferred_element_type=jnp.float32
    )
    return (squares_a[:, None] + squares_b[None, :] - 2.0 * product) / points_a.shape[1]


def combine(early, later):
    top = jnp.maximum(early[0], later[0])
    return (top, early[1] * jnp.exp(early[0] - top) + later[1] * jnp.exp(later[0] - top))


def body(src_points, tgt_points, log_src_mass, log_tgt_mass):
    targets = gathered_copies(tgt_points, ROW, 0)
    sqy = jnp.sum(targets.astype(jnp.float32) ** 2, axis=1)
    count = src_points.shape[0]
    block = min(256, count)
    blocks = count // block
    src_blocks = src_points.reshape(blocks, block, -1)
    sq_blocks = jnp.sum(src_points.astype(jnp.float32) ** 2, axis=1).reshape(blocks, block)
    mass_blocks = log_src_mass.reshape(blocks, block)
    width_tgt = targets.shape[0]
    tgt_potential = jnp.zeros((width_tgt,), jnp.float32)
    src_potential = jnp.zeros((count,), jnp.float32)
    for step in range(ITERS):

        def row_terms(points, squares):
            cost = cost_block(points, squares, targets, sqy)
            return log_tgt_mass[None, :] + (tgt_potential[None, :] - cost) / entropy_weight

        def row_pair(item):
            terms = row_terms(item[0], item[1])
            top = jnp.max(terms, axis=1)
            return (top, jnp.sum(jnp.exp(terms - top[:, None]), axis=1))

        top, total = lax.map(row_pair, (src_blocks, sq_blocks))
        top, total = combined_all((top.reshape(-1), total.reshape(-1)), COL, combine)
        src_potential = -entropy_weight * (top + jnp.log(total))
        pot_blocks = src_potential.reshape(blocks, block)

        def col_terms(points, squares, mass, pot):
            cost = cost_block(points, squares, targets, sqy)
            return mass[:, None] + (pot[:, None] - cost) / entropy_weight

        def pair_step(carry, item):
            terms = col_terms(item[0], item[1], item[2], item[3])
            block_top = jnp.max(terms, axis=0)
            block_sum = jnp.sum(jnp.exp(terms - block_top[None, :]), axis=0)
            return (combine(carry, (block_top, block_sum)), None)

        start = (
            jnp.full((width_tgt,), -jnp.inf, jnp.float32),
            jnp.zeros((width_tgt,), jnp.float32),
        )
        inputs = (src_blocks, sq_blocks, mass_blocks, pot_blocks)
        (top, total), unused = lax.scan(pair_step, start, inputs)
        top, total = joined_all((top, total), ROW, combine)
        tgt_potential = -entropy_weight * (top + jnp.log(total))
    sources_all = count * lax.axis_size(ROW)
    targets_all = width_tgt * lax.axis_size(COL)
    local = jnp.sum(src_potential) / (sources_all * lax.axis_size(COL)) + jnp.sum(tgt_potential) / (
        targets_all * lax.axis_size(ROW)
    )
    mean_potentials = over_axes(local, ROW_COL)
    return (src_potential, tgt_potential, mean_potentials)


def solution(mesh):
    finer = Mesh(mesh.devices.reshape(4, 4, 4, 2), ("row_0", "row_1", "col_0", "col_1"))
    placed = (P(ROW, None), P(COL_ROW, None), P(ROW), P(COL))
    return jax.shard_map(
        body, mesh=finer, in_specs=placed, out_specs=(P(ROW), P(COL), P()), check_vma=False
    )
```

profile of v0, /device:TPU:1, one launch (start us, length us, event | category | flops | bytes accessed | tf_op | source)
XLA Modules:
  0.0 220.8 jit_solution(14711009485905905026)
XLA Ops:
  0.7 2.5 %broadcast_in_dim.47 = bf16[16,256,256]{2,1,0:T(8,128)(2,1)} broadcast(bf16[256,256]{1,0:T(8,128)(2,1)} %param.17), dimensions={1,2} | broadcast | bytes 2228224 | tf_op jit(solution)/shard_map/broadcast_in_dim | solution.py:18
  3.2 7.6 %all-to-all-start = ((bf16[16,256,256]{2,1,0:T(8,128)(2,1)}), bf16[16,256,256]{2,1,0:T(8,128)(2,1)S(1)}, u32[]{:S(2)}, u32[]{:S(2)}) async-start(bf16[16,256,256]{2,1,0:T(8,128)(2,1)} %broadcast_in_dim.47), calls=%async_computation | async-start | bytes 4194304 | tf_op jit(solution)/shard_map/all_to_all | solution.py:17
  11.0 30.2 %all-to-all-done = bf16[16,256,256]{2,1,0:T(8,128)(2,1)S(1)} async-done(((bf16[16,256,256]{2,1,0:T(8,128)(2,1)}), bf16[16,256,256]{2,1,0:T(8,128)(2,1)S(1)}, u32[]{:S(2)}, u32[]{:S(2)}) %all-to-all-start) | async-done | bytes 2097184 | tf_op jit(solution)/shard_map/all_to_all | solution.py:17
  41.9 9.3 %while.75 = (s32[]{:T(128)}, f32[4,256]{1,0:T(4,128)S(1)}, f32[4,256]{1,0:T(4,128)S(1)}, f32[4096]{0:T(1024)S(1)}, f32[4,256]{1,0:T(4,128)S(1)}, /*index=5*/f32[...) while((s32[]{:T(128)}, f32[4,256]{1,0:T(4,128)S(1)}, ...), condition=%wide.region_5.6_spmd, body=%wide.region_2.5_spmd.sunk | while | flops 547356160 | bytes 10659957 | solution.py:125
  51.9 7.4 %all-to-all-start.1 = ((f32[8,2,1024]{2,1,0:T(2,128)}), f32[8,2,1024]{2,1,0:T(2,128)S(1)}, u32[]{:S(2)}, u32[]{:S(2)}) async-start(f32[8,2,1024]{2,1,0:T(2,128)} %broadcast_in_dim.48), calls=%async_computation.1 | async-start | bytes 131072 | tf_op jit(solution)/shard_map/all_to_all | solution.py:17
  59.4 4.8 %all-to-all-done.1 = f32[8,2,1024]{2,1,0:T(2,128)S(1)} async-done(((f32[8,2,1024]{2,1,0:T(2,128)}), f32[8,2,1024]{2,1,0:T(2,128)S(1)}, u32[]{:S(2)}, u32[]{:S(2)}) %all-to-all-start.1) | async-done | bytes 65568 | tf_op jit(solution)/shard_map/all_to_all | solution.py:17
  64.6 8.5 %while.78 = (s32[]{:T(128)}, f32[4096]{0:T(1024)S(1)}, f32[4096]{0:T(1024)S(1)}, f32[4,256]{1,0:T(4,128)S(1)}, f32[4,256]{1,0:T(4,128)S(1)}, /*index=5*/f32[4,25...) while((s32[]{:T(128)}, f32[4096]{0:T(1024)S(1)}, ...), condition=%wide.region_9.10_spmd.clone, body=%wide.region_6.9_spmd.clone.sunk | while | flops 547381248 | bytes 10790019 | solution.py:145
  74.1 3.6 %all-to-all-start.2 = ((f32[16,2,4096]{2,1,0:T(2,128)}), f32[16,2,4096]{2,1,0:T(2,128)S(1)}, u32[]{:S(2)}, u32[]{:S(2)}) async-start(f32[16,2,4096]{2,1,0:T(2,128)} %broadcast_in_dim.49), calls=%async_computation.2 | async-start | bytes 1048576 | tf_op jit(solution)/shard_map/all_to_all | solution.py:17
  77.7 10.5 %all-to-all-done.2 = f32[16,2,4096]{2,1,0:T(2,128)S(1)} async-done(((f32[16,2,4096]{2,1,0:T(2,128)}), f32[16,2,4096]{2,1,0:T(2,128)S(1)}, u32[]{:S(2)}, u32[]{:S(2)}) %all-to-all-start.2) | async-done | bytes 524320 | tf_op jit(solution)/shard_map/all_to_all | solution.py:17
  90.8 9.4 %while.76 = (s32[]{:T(128)}, f32[4,256]{1,0:T(4,128)S(1)}, f32[4,256]{1,0:T(4,128)S(1)}, f32[4096]{0:T(1024)S(1)}, f32[4096]{0:T(1024)S(1)}, /*index=5*/f32[4,25...) while((s32[]{:T(128)}, f32[4,256]{1,0:T(4,128)S(1)}, ...), condition=%wide.region_13.14_spmd, body=%wide.region_10.13_spmd.sunk | while | flops 547356160 | bytes 10676349 | solution.py:125
  90.8 1.5 fusion.101
  93.2 1.5 fusion.101
  95.5 1.5 fusion.101
  100.8 5.2 %all-to-all-start.3 = ((f32[8,2,1024]{2,1,0:T(2,128)}), f32[8,2,1024]{2,1,0:T(2,128)S(1)}, u32[]{:S(2)}, u32[]{:S(2)}) async-start(f32[8,2,1024]{2,1,0:T(2,128)} %broadcast_in_dim.50), calls=%async_computation.3 | async-start | bytes 131072 | tf_op jit(solution)/shard_map/all_to_all | solution.py:17
  106.0 4.9 %all-to-all-done.3 = f32[8,2,1024]{2,1,0:T(2,128)S(1)} async-done(((f32[8,2,1024]{2,1,0:T(2,128)}), f32[8,2,1024]{2,1,0:T(2,128)S(1)}, u32[]{:S(2)}, u32[]{:S(2)}) %all-to-all-start.3) | async-done | bytes 65568 | tf_op jit(solution)/shard_map/all_to_all | solution.py:17
  111.3 8.5 %while.79 = (s32[]{:T(128)}, f32[4096]{0:T(1024)S(1)}, f32[4096]{0:T(1024)S(1)}, f32[4,256]{1,0:T(4,128)S(1)}, f32[4,256]{1,0:T(4,128)S(1)}, /*index=5*/f32[4,25...) while((s32[]{:T(128)}, f32[4096]{0:T(1024)S(1)}, ...), condition=%wide.region_17.18_spmd.clone, body=%wide.region_14.17_spmd.clone.sunk | while | flops 547381248 | bytes 10790019 | solution.py:145
  120.8 3.6 %all-to-all-start.4 = ((f32[16,2,4096]{2,1,0:T(2,128)}), f32[16,2,4096]{2,1,0:T(2,128)S(1)}, u32[]{:S(2)}, u32[]{:S(2)}) async-start(f32[16,2,4096]{2,1,0:T(2,128)} %broadcast_in_dim.56), calls=%async_computation.4 | async-start | bytes 1048576 | tf_op jit(solution)/shard_map/all_to_all | solution.py:17
  124.4 10.5 %all-to-all-done.4 = f32[16,2,4096]{2,1,0:T(2,128)S(1)} async-done(((f32[16,2,4096]{2,1,0:T(2,128)}), f32[16,2,4096]{2,1,0:T(2,128)S(1)}, u32[]{:S(2)}, u32[]{:S(2)}) %all-to-all-start.4) | async-done | bytes 524320 | tf_op jit(solution)/shard_map/all_to_all | solution.py:17
  137.5 9.4 %while.77 = (s32[]{:T(128)}, f32[4,256]{1,0:T(4,128)S(1)}, f32[4,256]{1,0:T(4,128)S(1)}, f32[4096]{0:T(1024)S(1)}, f32[4096]{0:T(1024)S(1)}, /*index=5*/f32[4,25...) while((s32[]{:T(128)}, f32[4,256]{1,0:T(4,128)S(1)}, ...), condition=%wide.region_21.22_spmd, body=%wide.region_18.21_spmd.sunk | while | flops 547356160 | bytes 10676349 | solution.py:125
  139.9 1.5 fusion.103
  142.2 1.5 fusion.103
  144.6 1.5 fusion.103
  147.6 5.2 %all-to-all-start.5 = ((f32[8,2,1024]{2,1,0:T(2,128)}), f32[8,2,1024]{2,1,0:T(2,128)S(1)}, u32[]{:S(2)}, u32[]{:S(2)}) async-start(f32[8,2,1024]{2,1,0:T(2,128)} %broadcast_in_dim.57), calls=%async_computation.5 | async-start | bytes 131072 | tf_op jit(solution)/shard_map/all_to_all | solution.py:17
  152.7 4.9 %all-to-all-done.5 = f32[8,2,1024]{2,1,0:T(2,128)S(1)} async-done(((f32[8,2,1024]{2,1,0:T(2,128)}), f32[8,2,1024]{2,1,0:T(2,128)S(1)}, u32[]{:S(2)}, u32[]{:S(2)}) %all-to-all-start.5) | async-done | bytes 65568 | tf_op jit(solution)/shard_map/all_to_all | solution.py:17
  158.5 1.9 fusion.63
  160.3 8.4 %while.80 = (s32[]{:T(128)}, f32[4096]{0:T(1024)S(1)}, f32[4096]{0:T(1024)S(1)}, f32[4,256]{1,0:T(4,128)S(1)}, f32[4,256]{1,0:T(4,128)S(1)}, /*index=5*/f32[4,25...) while((s32[]{:T(128)}, f32[4096]{0:T(1024)S(1)}, ...), condition=%wide.region_25.26_spmd.clone, body=%wide.region_22.25_spmd.clone.sunk | while | flops 547381248 | bytes 10790019 | solution.py:145
  169.8 3.6 %all-to-all-start.6 = ((f32[16,2,4096]{2,1,0:T(2,128)}), f32[16,2,4096]{2,1,0:T(2,128)S(1)}, u32[]{:S(2)}, u32[]{:S(2)}) async-start(f32[16,2,4096]{2,1,0:T(2,128)} %broadcast_in_dim.58), calls=%async_computation.6 | async-start | bytes 1048576 | tf_op jit(solution)/shard_map/all_to_all | solution.py:17
  174.0 9.9 %all-to-all-done.6 = f32[16,2,4096]{2,1,0:T(2,128)S(1)} async-done(((f32[16,2,4096]{2,1,0:T(2,128)}), f32[16,2,4096]{2,1,0:T(2,128)S(1)}, u32[]{:S(2)}, u32[]{:S(2)}) %all-to-all-start.6) | async-done | bytes 524320 | tf_op jit(solution)/shard_map/all_to_all | solution.py:17
  188.3 7.2 %psum.28 = f32[]{:T(128)} all-reduce(f32[]{:T(128)S(6)} %add.300), channel_id=1, replica_groups=mesh['row_0'=4,'row_1'=4,'col_0'=4,'col_1'=2] {'row_0'}, use_global_device_ids=true, to_apply=%region_28.29 | all-reduce | flops 1 | bytes 8 | tf_op jit(solution)/shard_map/psum | solution.py:86
  195.5 7.4 %psum.29 = f32[]{:T(128)} all-reduce(f32[]{:T(128)} %psum.28), channel_id=1, replica_groups=mesh['row_0'=4,'row_1'=4,'col_0'=4,'col_1'=2] {'row_1'}, use_global_device_ids=true, to_apply=%region_29.30 | all-reduce | flops 1 | bytes 8 | tf_op jit(solution)/shard_map/psum | solution.py:86
  202.9 7.5 %psum.30 = f32[]{:T(128)} all-reduce(f32[]{:T(128)} %psum.29), channel_id=1, replica_groups=mesh['row_0'=4,'row_1'=4,'col_0'=4,'col_1'=2] {'col_0'}, use_global_device_ids=true, to_apply=%region_30.31 | all-reduce | flops 1 | bytes 8 | tf_op jit(solution)/shard_map/psum | solution.py:86
  210.4 10.4 %psum.31 = f32[]{:T(128)} all-reduce(f32[]{:T(128)} %psum.30), channel_id=1, replica_groups=mesh['row_0'=4,'row_1'=4,'col_0'=4,'col_1'=2] {'col_1'}, use_global_device_ids=true, to_apply=%region_31.32 | all-reduce | flops 1 | bytes 8 | tf_op jit(solution)/shard_map/psum | solution.py:86
  (256 shorter events, 59.4 us)
Async XLA Ops:
  0.6 10.1 %copy-start = (bf16[1024,256]{1,0:T(8,128)(2,1)S(1)}, bf16[1024,256]{1,0:T(8,128)(2,1)}, u32[]{:S(2)}) copy-start(bf16[1024,256]{1,0:T(8,128)(2,1)} %param.16) | copy-start | bytes 1572868
  0.6 41.3 %copy-start.2 = (f32[4096]{0:T(1024)S(1)}, f32[4096]{0:T(1024)}, u32[]{:S(2)}) copy-start(f32[4096]{0:T(1024)} %param.19) | copy-start | bytes 49156
  3.2 38.1 %all-to-all-start = ((bf16[16,256,256]{2,1,0:T(8,128)(2,1)}), bf16[16,256,256]{2,1,0:T(8,128)(2,1)S(1)}, u32[]{:S(2)}, u32[]{:S(2)}) async-start(bf16[16,256,256]{2,1,0:T(8,128)(2,1)} %broadcast_in_dim.47), calls=%async_computation | async-start | bytes 4194304 | tf_op jit(solution)/shard_map/all_to_all | solution.py:17
  41.9 17.4 %copy-start.1 = (f32[1024]{0:T(1024)S(1)}, f32[1024]{0:T(1024)}, u32[]{:S(2)}) copy-start(f32[1024]{0:T(1024)} %param.18) | copy-start | bytes 12292
  51.9 12.3 %all-to-all-start.1 = ((f32[8,2,1024]{2,1,0:T(2,128)}), f32[8,2,1024]{2,1,0:T(2,128)S(1)}, u32[]{:S(2)}, u32[]{:S(2)}) async-start(f32[8,2,1024]{2,1,0:T(2,128)} %broadcast_in_dim.48), calls=%async_computation.1 | async-start | bytes 131072 | tf_op jit(solution)/shard_map/all_to_all | solution.py:17
  74.1 14.1 %all-to-all-start.2 = ((f32[16,2,4096]{2,1,0:T(2,128)}), f32[16,2,4096]{2,1,0:T(2,128)S(1)}, u32[]{:S(2)}, u32[]{:S(2)}) async-start(f32[16,2,4096]{2,1,0:T(2,128)} %broadcast_in_dim.49), calls=%async_computation.2 | async-start | bytes 1048576 | tf_op jit(solution)/shard_map/all_to_all | solution.py:17
  100.8 10.1 %all-to-all-start.3 = ((f32[8,2,1024]{2,1,0:T(2,128)}), f32[8,2,1024]{2,1,0:T(2,128)S(1)}, u32[]{:S(2)}, u32[]{:S(2)}) async-start(f32[8,2,1024]{2,1,0:T(2,128)} %broadcast_in_dim.50), calls=%async_computation.3 | async-start | bytes 131072 | tf_op jit(solution)/shard_map/all_to_all | solution.py:17
  120.8 14.1 %all-to-all-start.4 = ((f32[16,2,4096]{2,1,0:T(2,128)}), f32[16,2,4096]{2,1,0:T(2,128)S(1)}, u32[]{:S(2)}, u32[]{:S(2)}) async-start(f32[16,2,4096]{2,1,0:T(2,128)} %broadcast_in_dim.56), calls=%async_computation.4 | async-start | bytes 1048576 | tf_op jit(solution)/shard_map/all_to_all | solution.py:17
  147.6 10.0 %all-to-all-start.5 = ((f32[8,2,1024]{2,1,0:T(2,128)}), f32[8,2,1024]{2,1,0:T(2,128)S(1)}, u32[]{:S(2)}, u32[]{:S(2)}) async-start(f32[8,2,1024]{2,1,0:T(2,128)} %broadcast_in_dim.57), calls=%async_computation.5 | async-start | bytes 131072 | tf_op jit(solution)/shard_map/all_to_all | solution.py:17
  169.8 14.1 %all-to-all-start.6 = ((f32[16,2,4096]{2,1,0:T(2,128)}), f32[16,2,4096]{2,1,0:T(2,128)S(1)}, u32[]{:S(2)}, u32[]{:S(2)}) async-start(f32[16,2,4096]{2,1,0:T(2,128)} %broadcast_in_dim.58), calls=%async_computation.6 | async-start | bytes 1048576 | tf_op jit(solution)/shard_map/all_to_all | solution.py:17
where the time goes:
time: 222 us; the launch traced here: 221 us
  waiting for transfers between devices  75.8 us (34%)
  starting transfers between devices  36.1 us (16%)
  matrix products  35.4 us (16%)
  blocking collectives  32.4 us (15%)
  other arithmetic  21 us (9%)
  local copies, waits for them, and re-layouts  16.5 us (7%)
  between operations  2.76 us (1%)
    all_to_all x7, waiting for transfers between devices, from_everyone(): lax.all_to_all(jnp.broadcast_to(value[None], (peers, *value.shape)), axis...  75.8 us
    all_to_all x7, starting transfers between devices, from_everyone(): lax.all_to_all(jnp.broadcast_to(value[None], (peers, *value.shape)), axis...  36.1 us
    dot_general x24, matrix products, cost_block(): lax.dot_general(points_a, points_b, (((1,), (1,)), ((), ())), preferred_e...  35.4 us
    psum x4, blocking collectives, over_axes(): value = lax.psum(value, axis)  32.4 us
    reduce_sum x12, other arithmetic, row_pair(): return (top, jnp.sum(jnp.exp(terms - top[:, None]), axis=1))  8.61 us
    broadcast_in_dim x7, local copies, waits for them, and re-layouts, from_everyone(): jnp.broadcast_to(value[None], (peers, *value.shape))  7.4 us
    reduce_sum x12, other arithmetic, pair_step(): block_sum = jnp.sum(jnp.exp(terms - block_top[None, :]), axis=0)  7.15 us
  transfers between devices with their start and end apart: 7, of which 7 were waited for; matrix products, arithmetic and copies ran while one was open for 0% of the time, Pallas kernels for 0%

commit v1 on v0

--- a/solution.py
+++ b/solution.py
@@ -83,7 +83,8 @@
 
 def over_axes(value, axes):
     for axis in axes:
-        value = lax.psum(value, axis)
+        parts = lax.all_gather(value, axis, axis=0, tiled=False)
+        value = parts.sum(axis=0)
     return value
 
 

time: 222 us -> 229 us (1.032)
  local copies, waits for them, and re-layouts: 16.5 us -> 24.3 us
  other arithmetic: 21 us -> 23.4 us
  blocking collectives: 32.4 us -> 30 us
    psum x4 -> x0, blocking collectives: 32.4 us -> none  [over_axes(): value = lax.psum(value, axis)]
    unnamed x0 -> x4, blocking collectives: none -> 30 us
    unnamed x23 -> x43, local copies, waits for them, and re-layouts: 1.04 us -> 8.85 us
    reduce_sum x0 -> x4, other arithmetic: none -> 2.41 us  [over_axes(): value = parts.sum(axis=0)]
where the time goes in v1:
time: 229 us; the launch traced here: 228 us
  waiting for transfers between devices  75.1 us (33%)
  starting transfers between devices  36.1 us (16%)
  matrix products  35.4 us (15%)
  blocking collectives  30 us (13%)
  local copies, waits for them, and re-layouts  24.3 us (11%)
  other arithmetic  23.4 us (10%)
  between operations  2.82 us (1%)
    all_to_all x7, waiting for transfers between devices, from_everyone(): lax.all_to_all(jnp.broadcast_to(value[None], (peers, *value.shape)), axis...  75.1 us
    all_to_all x7, starting transfers between devices, from_everyone(): lax.all_to_all(jnp.broadcast_to(value[None], (peers, *value.shape)), axis...  36.1 us
    dot_general x24, matrix products, cost_block(): lax.dot_general(points_a, points_b, (((1,), (1,)), ((), ())), preferred_e...  35.4 us
    unnamed x4, blocking collectives  30 us
    unnamed x43, local copies, waits for them, and re-layouts  8.85 us
    reduce_sum x12, other arithmetic, row_pair(): return (top, jnp.sum(jnp.exp(terms - top[:, None]), axis=1))  8.61 us
    broadcast_in_dim x7, local copies, waits for them, and re-layouts, from_everyone(): jnp.broadcast_to(value[None], (peers, *value.shape))  7.4 us
    reduce_sum x12, other arithmetic, pair_step(): block_sum = jnp.sum(jnp.exp(terms - block_top[None, :]), axis=0)  7.15 us
  transfers between devices with their start and end apart: 7, of which 7 were waited for; matrix products, arithmetic and copies ran while one was open for 0% of the time, Pallas kernels for 0%

profile of v1, /device:TPU:1, one launch (start us, length us, event | category | flops | bytes accessed | tf_op | source)
XLA Modules:
  0.0 227.9 jit_solution(1655684943578808172)
XLA Ops:
  0.7 2.5 %broadcast_in_dim.47 = bf16[16,256,256]{2,1,0:T(8,128)(2,1)} broadcast(bf16[256,256]{1,0:T(8,128)(2,1)} %param.17), dimensions={1,2} | broadcast | bytes 2228224 | tf_op jit(solution)/shard_map/broadcast_in_dim | solution.py:18
  3.2 7.6 %all-to-all-start = ((bf16[16,256,256]{2,1,0:T(8,128)(2,1)}), bf16[16,256,256]{2,1,0:T(8,128)(2,1)S(1)}, u32[]{:S(2)}, u32[]{:S(2)}) async-start(bf16[16,256,256]{2,1,0:T(8,128)(2,1)} %broadcast_in_dim.47), calls=%async_computation | async-start | bytes 4194304 | tf_op jit(solution)/shard_map/all_to_all | solution.py:17
  11.0 30.2 %all-to-all-done = bf16[16,256,256]{2,1,0:T(8,128)(2,1)S(1)} async-done(((bf16[16,256,256]{2,1,0:T(8,128)(2,1)}), bf16[16,256,256]{2,1,0:T(8,128)(2,1)S(1)}, u32[]{:S(2)}, u32[]{:S(2)}) %all-to-all-start) | async-done | bytes 2097184 | tf_op jit(solution)/shard_map/all_to_all | solution.py:17
  41.9 9.3 %while.75 = (s32[]{:T(128)}, f32[4,256]{1,0:T(4,128)S(1)}, f32[4,256]{1,0:T(4,128)S(1)}, f32[4096]{0:T(1024)S(1)}, f32[4,256]{1,0:T(4,128)S(1)}, /*index=5*/f32[...) while((s32[]{:T(128)}, f32[4,256]{1,0:T(4,128)S(1)}, ...), condition=%wide.region_5.6_spmd, body=%wide.region_2.5_spmd.sunk | while | flops 547356160 | bytes 10659957 | solution.py:126
  51.9 7.4 %all-to-all-start.1 = ((f32[8,2,1024]{2,1,0:T(2,128)}), f32[8,2,1024]{2,1,0:T(2,128)S(1)}, u32[]{:S(2)}, u32[]{:S(2)}) async-start(f32[8,2,1024]{2,1,0:T(2,128)} %broadcast_in_dim.48), calls=%async_computation.1 | async-start | bytes 131072 | tf_op jit(solution)/shard_map/all_to_all | solution.py:17
  59.4 4.8 %all-to-all-done.1 = f32[8,2,1024]{2,1,0:T(2,128)S(1)} async-done(((f32[8,2,1024]{2,1,0:T(2,128)}), f32[8,2,1024]{2,1,0:T(2,128)S(1)}, u32[]{:S(2)}, u32[]{:S(2)}) %all-to-all-start.1) | async-done | bytes 65568 | tf_op jit(solution)/shard_map/all_to_all | solution.py:17
  64.6 8.5 %while.78 = (s32[]{:T(128)}, f32[4096]{0:T(1024)S(1)}, f32[4096]{0:T(1024)S(1)}, f32[4,256]{1,0:T(4,128)S(1)}, f32[4,256]{1,0:T(4,128)S(1)}, /*index=5*/f32[4,25...) while((s32[]{:T(128)}, f32[4096]{0:T(1024)S(1)}, ...), condition=%wide.region_9.10_spmd.clone, body=%wide.region_6.9_spmd.clone.sunk | while | flops 547381248 | bytes 10790019 | solution.py:146
  74.1 3.6 %all-to-all-start.2 = ((f32[16,2,4096]{2,1,0:T(2,128)}), f32[16,2,4096]{2,1,0:T(2,128)S(1)}, u32[]{:S(2)}, u32[]{:S(2)}) async-start(f32[16,2,4096]{2,1,0:T(2,128)} %broadcast_in_dim.49), calls=%async_computation.2 | async-start | bytes 1048576 | tf_op jit(solution)/shard_map/all_to_all | solution.py:17
  77.7 10.5 %all-to-all-done.2 = f32[16,2,4096]{2,1,0:T(2,128)S(1)} async-done(((f32[16,2,4096]{2,1,0:T(2,128)}), f32[16,2,4096]{2,1,0:T(2,128)S(1)}, u32[]{:S(2)}, u32[]{:S(2)}) %all-to-all-start.2) | async-done | bytes 524320 | tf_op jit(solution)/shard_map/all_to_all | solution.py:17
  90.8 9.4 %while.76 = (s32[]{:T(128)}, f32[4,256]{1,0:T(4,128)S(1)}, f32[4,256]{1,0:T(4,128)S(1)}, f32[4096]{0:T(1024)S(1)}, f32[4096]{0:T(1024)S(1)}, /*index=5*/f32[4,25...) while((s32[]{:T(128)}, f32[4,256]{1,0:T(4,128)S(1)}, ...), condition=%wide.region_13.14_spmd, body=%wide.region_10.13_spmd.sunk | while | flops 547356160 | bytes 10676349 | solution.py:126
  90.8 1.5 fusion.101
  93.2 1.5 fusion.101
  95.5 1.5 fusion.101
  100.8 5.2 %all-to-all-start.3 = ((f32[8,2,1024]{2,1,0:T(2,128)}), f32[8,2,1024]{2,1,0:T(2,128)S(1)}, u32[]{:S(2)}, u32[]{:S(2)}) async-start(f32[8,2,1024]{2,1,0:T(2,128)} %broadcast_in_dim.50), calls=%async_computation.3 | async-start | bytes 131072 | tf_op jit(solution)/shard_map/all_to_all | solution.py:17
  106.0 4.9 %all-to-all-done.3 = f32[8,2,1024]{2,1,0:T(2,128)S(1)} async-done(((f32[8,2,1024]{2,1,0:T(2,128)}), f32[8,2,1024]{2,1,0:T(2,128)S(1)}, u32[]{:S(2)}, u32[]{:S(2)}) %all-to-all-start.3) | async-done | bytes 65568 | tf_op jit(solution)/shard_map/all_to_all | solution.py:17
  111.3 8.5 %while.79 = (s32[]{:T(128)}, f32[4096]{0:T(1024)S(1)}, f32[4096]{0:T(1024)S(1)}, f32[4,256]{1,0:T(4,128)S(1)}, f32[4,256]{1,0:T(4,128)S(1)}, /*index=5*/f32[4,25...) while((s32[]{:T(128)}, f32[4096]{0:T(1024)S(1)}, ...), condition=%wide.region_17.18_spmd.clone, body=%wide.region_14.17_spmd.clone.sunk | while | flops 547381248 | bytes 10790019 | solution.py:146
  120.8 3.6 %all-to-all-start.4 = ((f32[16,2,4096]{2,1,0:T(2,128)}), f32[16,2,4096]{2,1,0:T(2,128)S(1)}, u32[]{:S(2)}, u32[]{:S(2)}) async-start(f32[16,2,4096]{2,1,0:T(2,128)} %broadcast_in_dim.56), calls=%async_computation.4 | async-start | bytes 1048576 | tf_op jit(solution)/shard_map/all_to_all | solution.py:17
  124.4 10.5 %all-to-all-done.4 = f32[16,2,4096]{2,1,0:T(2,128)S(1)} async-done(((f32[16,2,4096]{2,1,0:T(2,128)}), f32[16,2,4096]{2,1,0:T(2,128)S(1)}, u32[]{:S(2)}, u32[]{:S(2)}) %all-to-all-start.4) | async-done | bytes 524320 | tf_op jit(solution)/shard_map/all_to_all | solution.py:17
  137.5 9.4 %while.77 = (s32[]{:T(128)}, f32[4,256]{1,0:T(4,128)S(1)}, f32[4,256]{1,0:T(4,128)S(1)}, f32[4096]{0:T(1024)S(1)}, f32[4096]{0:T(1024)S(1)}, /*index=5*/f32[4,25...) while((s32[]{:T(128)}, f32[4,256]{1,0:T(4,128)S(1)}, ...), condition=%wide.region_21.22_spmd, body=%wide.region_18.21_spmd.sunk | while | flops 547356160 | bytes 10676349 | solution.py:126
  139.9 1.5 fusion.103
  142.2 1.5 fusion.103
  144.6 1.5 fusion.103
  147.6 5.2 %all-to-all-start.5 = ((f32[8,2,1024]{2,1,0:T(2,128)}), f32[8,2,1024]{2,1,0:T(2,128)S(1)}, u32[]{:S(2)}, u32[]{:S(2)}) async-start(f32[8,2,1024]{2,1,0:T(2,128)} %broadcast_in_dim.57), calls=%async_computation.5 | async-start | bytes 131072 | tf_op jit(solution)/shard_map/all_to_all | solution.py:17
  152.7 4.9 %all-to-all-done.5 = f32[8,2,1024]{2,1,0:T(2,128)S(1)} async-done(((f32[8,2,1024]{2,1,0:T(2,128)}), f32[8,2,1024]{2,1,0:T(2,128)S(1)}, u32[]{:S(2)}, u32[]{:S(2)}) %all-to-all-start.5) | async-done | bytes 65568 | tf_op jit(solution)/shard_map/all_to_all | solution.py:17
  158.5 1.9 fusion.63
  160.3 8.5 %while.80 = (s32[]{:T(128)}, f32[4096]{0:T(1024)S(1)}, f32[4096]{0:T(1024)S(1)}, f32[4,256]{1,0:T(4,128)S(1)}, f32[4,256]{1,0:T(4,128)S(1)}, /*index=5*/f32[4,25...) while((s32[]{:T(128)}, f32[4096]{0:T(1024)S(1)}, ...), condition=%wide.region_25.26_spmd.clone, body=%wide.region_22.25_spmd.clone.sunk | while | flops 547381248 | bytes 10790019 | solution.py:146
  169.9 3.6 %all-to-all-start.6 = ((f32[16,2,4096]{2,1,0:T(2,128)}), f32[16,2,4096]{2,1,0:T(2,128)S(1)}, u32[]{:S(2)}, u32[]{:S(2)}) async-start(f32[16,2,4096]{2,1,0:T(2,128)} %broadcast_in_dim.58), calls=%async_computation.6 | async-start | bytes 1048576 | tf_op jit(solution)/shard_map/all_to_all | solution.py:17
  174.8 9.2 %all-to-all-done.6 = f32[16,2,4096]{2,1,0:T(2,128)S(1)} async-done(((f32[16,2,4096]{2,1,0:T(2,128)}), f32[16,2,4096]{2,1,0:T(2,128)S(1)}, u32[]{:S(2)}, u32[]{:S(2)}) %all-to-all-start.6) | async-done | bytes 524320 | tf_op jit(solution)/shard_map/all_to_all | solution.py:17
  189.9 6.7 %all-reduce = f32[4]{0:T(128)S(1)} all-reduce(f32[4]{0:T(128)S(1)} %dynamic-update-slice), channel_id=1, replica_groups=mesh['row_0'=4,'row_1'=4,'col_0'=4,'col_1'=2] {'row_0'}, use_global_device_ids=true, to_apply=%add | all-reduce | flops 4 | bytes 32
  199.2 6.7 %all-reduce.1 = f32[4]{0:T(128)S(1)} all-reduce(f32[4]{0:T(128)S(1)} %dynamic-update-slice.1), channel_id=1, replica_groups=mesh['row_0'=4,'row_1'=4,'col_0'=4,'col_1'=2] {'row_1'}, use_global_device_ids=true, to_apply=%add.1 | all-reduce | flops 4 | bytes 32
  208.7 6.8 %all-reduce.2 = f32[4]{0:T(128)S(1)} all-reduce(f32[4]{0:T(128)S(1)} %dynamic-update-slice.2), channel_id=1, replica_groups=mesh['row_0'=4,'row_1'=4,'col_0'=4,'col_1'=2] {'col_0'}, use_global_device_ids=true, to_apply=%add.2 | all-reduce | flops 4 | bytes 32
  217.6 9.8 %all-reduce.3 = f32[2]{0:T(128)S(1)} all-reduce(f32[2]{0:T(128)S(1)} %dynamic-update-slice.3), channel_id=1, replica_groups=mesh['row_0'=4,'row_1'=4,'col_0'=4,'col_1'=2] {'col_1'}, use_global_device_ids=true, to_apply=%add.3 | all-reduce | flops 2 | bytes 16
  (280 shorter events, 69.6 us)
Async XLA Ops:
  0.6 10.1 %copy-start = (bf16[1024,256]{1,0:T(8,128)(2,1)S(1)}, bf16[1024,256]{1,0:T(8,128)(2,1)}, u32[]{:S(2)}) copy-start(bf16[1024,256]{1,0:T(8,128)(2,1)} %param.16) | copy-start | bytes 1572868
  0.6 41.3 %copy-start.2 = (f32[4096]{0:T(1024)S(1)}, f32[4096]{0:T(1024)}, u32[]{:S(2)}) copy-start(f32[4096]{0:T(1024)} %param.19) | copy-start | bytes 49156
  3.2 38.1 %all-to-all-start = ((bf16[16,256,256]{2,1,0:T(8,128)(2,1)}), bf16[16,256,256]{2,1,0:T(8,128)(2,1)S(1)}, u32[]{:S(2)}, u32[]{:S(2)}) async-start(bf16[16,256,256]{2,1,0:T(8,128)(2,1)} %broadcast_in_dim.47), calls=%async_computation | async-start | bytes 4194304 | tf_op jit(solution)/shard_map/all_to_all | solution.py:17
  41.9 17.4 %copy-start.1 = (f32[1024]{0:T(1024)S(1)}, f32[1024]{0:T(1024)}, u32[]{:S(2)}) copy-start(f32[1024]{0:T(1024)} %param.18) | copy-start | bytes 12292
  51.9 12.3 %all-to-all-start.1 = ((f32[8,2,1024]{2,1,0:T(2,128)}), f32[8,2,1024]{2,1,0:T(2,128)S(1)}, u32[]{:S(2)}, u32[]{:S(2)}) async-start(f32[8,2,1024]{2,1,0:T(2,128)} %broadcast_in_dim.48), calls=%async_computation.1 | async-start | bytes 131072 | tf_op jit(solution)/shard_map/all_to_all | solution.py:17
  74.1 14.1 %all-to-all-start.2 = ((f32[16,2,4096]{2,1,0:T(2,128)}), f32[16,2,4096]{2,1,0:T(2,128)S(1)}, u32[]{:S(2)}, u32[]{:S(2)}) async-start(f32[16,2,4096]{2,1,0:T(2,128)} %broadcast_in_dim.49), calls=%async_computation.2 | async-start | bytes 1048576 | tf_op jit(solution)/shard_map/all_to_all | solution.py:17
  100.8 10.1 %all-to-all-start.3 = ((f32[8,2,1024]{2,1,0:T(2,128)}), f32[8,2,1024]{2,1,0:T(2,128)S(1)}, u32[]{:S(2)}, u32[]{:S(2)}) async-start(f32[8,2,1024]{2,1,0:T(2,128)} %broadcast_in_dim.50), calls=%async_computation.3 | async-start | bytes 131072 | tf_op jit(solution)/shard_map/all_to_all | solution.py:17
  120.8 14.1 %all-to-all-start.4 = ((f32[16,2,4096]{2,1,0:T(2,128)}), f32[16,2,4096]{2,1,0:T(2,128)S(1)}, u32[]{:S(2)}, u32[]{:S(2)}) async-start(f32[16,2,4096]{2,1,0:T(2,128)} %broadcast_in_dim.56), calls=%async_computation.4 | async-start | bytes 1048576 | tf_op jit(solution)/shard_map/all_to_all | solution.py:17
  147.6 10.0 %all-to-all-start.5 = ((f32[8,2,1024]{2,1,0:T(2,128)}), f32[8,2,1024]{2,1,0:T(2,128)S(1)}, u32[]{:S(2)}, u32[]{:S(2)}) async-start(f32[8,2,1024]{2,1,0:T(2,128)} %broadcast_in_dim.57), calls=%async_computation.5 | async-start | bytes 131072 | tf_op jit(solution)/shard_map/all_to_all | solution.py:17
  160.3 13.1 %copy-start.6 = (u32[128]{0:T(128)S(1)}, u32[128]{0:T(128)}, u32[]{:S(2)}) copy-start(u32[128]{0:T(128)} %constant.149) | copy-start | bytes 1540
  168.8 20.4 %copy-start.5 = (u32[128]{0:T(128)S(1)}, u32[128]{0:T(128)}, u32[]{:S(2)}) copy-start(u32[128]{0:T(128)} %constant.154) | copy-start | bytes 1540
  168.8 29.8 %copy-start.4 = (u32[128]{0:T(128)S(1)}, u32[128]{0:T(128)}, u32[]{:S(2)}) copy-start(u32[128]{0:T(128)} %constant.159) | copy-start | bytes 1540
  168.8 39.2 %copy-start.3 = (u32[128]{0:T(128)S(1)}, u32[128]{0:T(128)}, u32[]{:S(2)}) copy-start(u32[128]{0:T(128)} %constant.164) | copy-start | bytes 1540
  169.9 14.1 %all-to-all-start.6 = ((f32[16,2,4096]{2,1,0:T(2,128)}), f32[16,2,4096]{2,1,0:T(2,128)S(1)}, u32[]{:S(2)}, u32[]{:S(2)}) async-start(f32[16,2,4096]{2,1,0:T(2,128)} %broadcast_in_dim.58), calls=%async_computation.6 | async-start | bytes 1048576 | tf_op jit(solution)/shard_map/all_to_all | solution.py:17
